TPU v7x, 256 devices: a whole 4x4x8 slice. The times are simulated.
256 devices in a mesh: dp: 16 (over z_lo, x), seq: 16 (over z_hi, y, core).
Axes of the slice: x: 4, y: 4, z: 8 (z_hi: 2, z_lo: 4; z = z_hi * 4 + z_lo), core: 2. Of those that a mesh axis runs over, the one named last changes fastest.
Arguments:
- queries: bfloat16 [16, 2048, 2048], P('dp', 'seq'), may hold values from -5 to 5
- key_states: bfloat16 [16, 2048, 2048], P('dp', 'seq'), may hold values from -5 to 5
- value_states: bfloat16 [16, 2048, 2048], P('dp', 'seq'), may hold values from -6 to 6
- residual: bfloat16 [16, 2048, 2048], P('dp', 'seq'), may hold values from -6 to 6
- enc_hidden: bfloat16 [16, 2048, 1536], P('dp', 'seq'), may hold values from -6 to 6
- enc_gain: float32 [1536], replicated, may hold values from 0.1 to 1.9
- enc_bias: float32 [1536], replicated, may hold values from -0.5 to 0.5
- feature_target: int32 [16, 2048], P('dp', 'seq'), may hold values from 0 to 2047, as said below
- timestep: int32 [16], P('dp'), may hold values from 0 to 999
- gate_weight: bfloat16 [256, 2048], P('dp'), may hold values from -0.375 to 0.375
- lift_weight: bfloat16 [2048, 1024], P('dp'), may hold values from -0.125 to 0.125
- out_weight: bfloat16 [1024, 1536], P('dp'), may hold values from -0.1875 to 0.1875
Outputs:
- d_queries: bfloat16 [16, 2048, 2048], P('dp', 'seq')
- d_keys: bfloat16 [16, 2048, 2048], P('dp', 'seq')
- d_values: bfloat16 [16, 2048, 2048], P('dp', 'seq')
- grad_gate: float32 [256, 2048], P('dp')
- grad_lift: float32 [2048, 1024], P('dp')
- grad_out: float32 [1024, 1536], P('dp')
Inputs may be any that keep to these rules, and one draw needn't show every extreme that they name: For each clip, feature_target is a permutation of its 2048 token positions. The 128 encoder rows of one device of seq target at most 16 tokens held by any one device of seq, and exactly 16 for some.
All inputs are finite; a program needn't handle non-finite values.
Results may differ from a plain program's by a relative error of at most 0.02.
Values may be sent and summed in bfloat16 or wider, within the bound.
A program may use at most 128 MiB of HBM per device.

v0:
```python
import math
import jax
import jax.numpy as jnp
from jax import lax
from jax.sharding import PartitionSpec as P

HD = 128
ZD = 1536
TEMB = 256
EPSILON = 1e-06


def laid_out(blocks, dim):
    blocks = jnp.moveaxis(blocks, 0, dim)
    lengths = blocks.shape
    return blocks.reshape(*lengths[:dim], lengths[dim] * lengths[dim + 1], *lengths[dim + 2 :])


def gather_packed(arrays, axis, dims):
    line = jnp.concatenate([a.reshape(-1) for a in arrays])
    lines, at, done = (lax.all_gather(line, axis), 0, [])
    for a, dim in zip(arrays, dims):
        blocks = lines[:, at : at + a.size].reshape(-1, *a.shape)
        done.append(laid_out(blocks, dim))
        at += a.size
    return tuple(done)


def embed_time(timestep):
    half_width = TEMB // 2
    frequency = jnp.exp(
        -math.log(10000.0) * jnp.arange(half_width).astype(jnp.float32) / half_width
    )
    angles = timestep.astype(jnp.float32)[:, None] * frequency[None, :]
    return jnp.concatenate([jnp.cos(angles), jnp.sin(angles)], axis=1).astype(jnp.bfloat16)


def encoder_norm(hidden, enc_gain, enc_bias):
    widened = hidden.astype(jnp.float32)
    centred = widened - jnp.mean(widened, axis=-1, keepdims=True)
    variance = jnp.mean(centred * centred, axis=-1, keepdims=True)
    return (centred * lax.rsqrt(variance + EPSILON) * enc_gain + enc_bias).astype(jnp.bfloat16)


def soft_scores(query_block, key_heads):
    scores = jnp.einsum(
        "bhd,lhd->hbl", query_block, key_heads, preferred_element_type=jnp.float32
    ) * HD ** (-0.5)
    shifted = jnp.exp(scores - jnp.max(scores, axis=-1, keepdims=True))
    return shifted / jnp.sum(shifted, axis=-1, keepdims=True)


def split_blocks(array):
    length = array.shape[0]
    block_rows = min(length, 512)
    return array.reshape(length // block_rows, block_rows, array.shape[1], array.shape[2])


def attention_forward(query_heads, key_heads, value_heads):

    def one_block(query_block):
        chances = soft_scores(query_block, key_heads).astype(jnp.bfloat16)
        return jnp.einsum(
            "hbl,lhd->bhd", chances, value_heads, preferred_element_type=jnp.float32
        ).astype(jnp.bfloat16)

    mixed = lax.map(one_block, split_blocks(query_heads))
    return mixed.reshape(query_heads.shape[0], -1)


def attention_backward(query_heads, key_heads, value_heads, grad_heads):

    def one_block(carried, pieces):
        grad_keys, grad_values = carried
        query_block, grad_block = pieces
        chances = soft_scores(query_block, key_heads)
        grad_chances = jnp.einsum(
            "bhd,lhd->hbl", grad_block, value_heads, preferred_element_type=jnp.float32
        )
        grad_values = grad_values + jnp.einsum(
            "hbl,bhd->lhd",
            chances.astype(jnp.bfloat16),
            grad_block,
            preferred_element_type=jnp.float32,
        )
        inner_sum = jnp.sum(grad_chances * chances, axis=-1, keepdims=True)
        grad_scores = (chances * (grad_chances - inner_sum) * HD ** (-0.5)).astype(jnp.bfloat16)
        grad_query = jnp.einsum(
            "hbl,lhd->bhd", grad_scores, key_heads, preferred_element_type=jnp.float32
        )
        grad_keys = grad_keys + jnp.einsum(
            "hbl,bhd->lhd", grad_scores, query_block, preferred_element_type=jnp.float32
        )
        return ((grad_keys, grad_values), grad_query.astype(jnp.bfloat16))

    zeros = jnp.zeros(key_heads.shape, jnp.float32)
    carried, grad_queries = lax.scan(
        one_block, (zeros, zeros), (split_blocks(query_heads), split_blocks(grad_heads))
    )
    length = query_heads.shape[0]
    return (
        grad_queries.reshape(length, -1),
        carried[0].reshape(length, -1).astype(jnp.bfloat16),
        carried[1].reshape(length, -1).astype(jnp.bfloat16),
    )


def shards(
    queries,
    key_states,
    value_states,
    residual,
    enc_hidden,
    enc_gain,
    enc_bias,
    feature_target,
    timestep,
    gate_weight,
    lift_weight,
    out_weight,
):
    groups = lax.axis_size("seq")
    tokens_here = queries.shape[1]
    z_width = enc_hidden.shape[2]
    capacity = 2 * tokens_here // groups
    normed = encoder_norm(enc_hidden[0], enc_gain, enc_bias)
    targets = feature_target[0]
    owning = targets // tokens_here
    onehot = (owning[:, None] == jnp.arange(groups)[None, :]).astype(jnp.int32)
    ranked = jnp.sum((jnp.cumsum(onehot, axis=0) - onehot) * onehot, axis=1)
    slotted = owning * capacity + ranked
    send_rows = jnp.zeros((groups * capacity, z_width), jnp.bfloat16).at[slotted].set(normed)
    send_places = (
        jnp.zeros((groups * capacity,), jnp.int32).at[slotted].set(targets % tokens_here + 1)
    )
    got_rows, got_places = (
        lax.all_to_all(
            send_rows.reshape(groups, capacity, z_width),
            "seq",
            split_axis=0,
            concat_axis=0,
            tiled=True,
        ),
        lax.all_to_all(
            send_places.reshape(groups, capacity), "seq", split_axis=0, concat_axis=0, tiled=True
        ),
    )
    aligned = (
        jnp.zeros((tokens_here + 1, z_width), jnp.bfloat16)
        .at[got_places.reshape(-1)]
        .set(got_rows.reshape(-1, z_width))[1:]
    )
    gate_full, lift_full, out_full = gather_packed(
        (gate_weight, lift_weight, out_weight), "dp", (0, 0, 0)
    )
    embedded = embed_time(timestep)
    gating = jnp.dot(embedded, gate_full, preferred_element_type=jnp.float32)
    query_heads, key_heads, value_heads = (
        lax.all_to_all(queries[0], "seq", split_axis=1, concat_axis=0, tiled=True),
        lax.all_to_all(key_states[0], "seq", split_axis=1, concat_axis=0, tiled=True),
        lax.all_to_all(value_states[0], "seq", split_axis=1, concat_axis=0, tiled=True),
    )
    local_width = query_heads.shape[1]

    def heads_of(array):
        return array.reshape(array.shape[0], local_width // HD, HD)

    mixed_heads = attention_forward(
        heads_of(query_heads), heads_of(key_heads), heads_of(value_heads)
    )
    mixed = lax.all_to_all(mixed_heads, "seq", split_axis=0, concat_axis=1, tiled=True)
    mixed_wide = mixed.astype(jnp.float32)
    hidden = (residual[0].astype(jnp.float32) + gating * mixed_wide).astype(jnp.bfloat16)
    lifted = jnp.dot(hidden, lift_full, preferred_element_type=jnp.float32)
    sigmoid_lift = jax.nn.sigmoid(lifted)
    activated = (lifted * sigmoid_lift).astype(jnp.bfloat16)
    predicted = jnp.dot(activated, out_full, preferred_element_type=jnp.float32)
    target_wide = aligned.astype(jnp.float32)
    pred_norm = jnp.sqrt(jnp.sum(predicted * predicted, axis=1, keepdims=True) + EPSILON)
    target_norm = jnp.sqrt(jnp.sum(target_wide * target_wide, axis=1, keepdims=True) + EPSILON)
    cosine = jnp.sum(predicted * target_wide, axis=1, keepdims=True) / (pred_norm * target_norm)
    grad_pred = (
        -1.0
        * ZD
        * (target_wide / (pred_norm * target_norm) - cosine * predicted / (pred_norm * pred_norm))
    ).astype(jnp.bfloat16)
    part_out = jnp.einsum("tp,tz->pz", activated, grad_pred, preferred_element_type=jnp.float32)
    grad_act = jnp.einsum("tz,pz->tp", grad_pred, out_full, preferred_element_type=jnp.float32)
    grad_lifted = (grad_act * sigmoid_lift * (1.0 + lifted * (1.0 - sigmoid_lift))).astype(
        jnp.bfloat16
    )
    part_lift = jnp.einsum("tf,tp->fp", hidden, grad_lifted, preferred_element_type=jnp.float32)
    grad_hidden = jnp.einsum(
        "tp,fp->tf", grad_lifted, lift_full, preferred_element_type=jnp.float32
    )
    grad_mixed = (gating * grad_hidden).astype(jnp.bfloat16)
    grad_gating = jnp.sum(grad_hidden * mixed_wide, axis=0, keepdims=True)
    part_gate = jnp.dot(
        embedded.astype(jnp.float32).T, grad_gating, precision=lax.Precision.HIGHEST
    )
    grad_heads = lax.all_to_all(grad_mixed, "seq", split_axis=1, concat_axis=0, tiled=True)
    grad_query, grad_key, grad_value = attention_backward(
        heads_of(query_heads), heads_of(key_heads), heads_of(value_heads), heads_of(grad_heads)
    )
    d_queries, d_keys, d_values = (
        lax.all_to_all(grad_query, "seq", split_axis=0, concat_axis=1, tiled=True),
        lax.all_to_all(grad_key, "seq", split_axis=0, concat_axis=1, tiled=True),
        lax.all_to_all(grad_value, "seq", split_axis=0, concat_axis=1, tiled=True),
    )
    share_gate, share_lift, share_out = (
        lax.psum_scatter(
            part_gate.astype(jnp.bfloat16), "dp", scatter_dimension=0, tiled=True
        ).astype(jnp.float32),
        lax.psum_scatter(
            part_lift.astype(jnp.bfloat16), "dp", scatter_dimension=0, tiled=True
        ).astype(jnp.float32),
        lax.psum_scatter(
            part_out.astype(jnp.bfloat16), "dp", scatter_dimension=0, tiled=True
        ).astype(jnp.float32),
    )
    grad_gate, grad_lift, grad_out = (
        lax.psum(share_gate.astype(jnp.bfloat16), "seq").astype(jnp.float32),
        lax.psum(share_lift.astype(jnp.bfloat16), "seq").astype(jnp.float32),
        lax.psum(share_out.astype(jnp.bfloat16), "seq").astype(jnp.float32),
    )
    return (d_queries[None], d_keys[None], d_values[None], grad_gate, grad_lift, grad_out)


def solution(mesh):
    in_specs = (
        P("dp", "seq", None),
        P("dp", "seq", None),
        P("dp", "seq", None),
        P("dp", "seq", None),
        P("dp", "seq", None),
        P(),
        P(),
        P("dp", "seq"),
        P("dp"),
        P("dp", None),
        P("dp", None),
        P("dp", None),
    )
    out_specs = (
        P("dp", "seq", None),
        P("dp", "seq", None),
        P("dp", "seq", None),
        P("dp", None),
        P("dp", None),
        P("dp", None),
    )
    return jax.shard_map(shards, mesh=mesh, in_specs=in_specs, out_specs=out_specs, check_vma=False)
```

profile of v0, /device:TPU:1, one launch (start us, length us, event | category | flops | bytes accessed | tf_op | source)
XLA Modules:
  0.0 702.5 jit_solution(1109292833867318314)
XLA Ops:
  11.3 2.0 copy.62
  13.3 12.6 %all-to-all-start = ((bf16[128,16,128]{0,2,1:T(8,128)(2,1)}), bf16[128,16,128]{0,2,1:T(8,128)(2,1)S(1)}, u32[]{:S(2)}, u32[]{:S(2)}) async-start(bf16[128,16,128]{0,2,1:T(8,128)(2,1)} %bitcast.7), calls=%async_computation | async-start | bytes 1048576 | tf_op jit(solution)/shard_map/all_to_all | solution.py:159
  26.9 20.7 %all-to-all-done = bf16[128,16,128]{0,2,1:T(8,128)(2,1)S(1)} async-done(((bf16[128,16,128]{0,2,1:T(8,128)(2,1)}), bf16[128,16,128]{0,2,1:T(8,128)(2,1)S(1)}, u32[]{:S(2)}, u32[]{:S(2)}) %all-to-all-start) | async-done | bytes 524320 | tf_op jit(solution)/shard_map/all_to_all | solution.py:159
  47.6 4.5 all-to-all-start.1
  53.1 17.1 %all-to-all-done.1 = bf16[128,16,128]{0,2,1:T(8,128)(2,1)S(1)} async-done(((bf16[128,16,128]{0,2,1:T(8,128)(2,1)}), bf16[128,16,128]{0,2,1:T(8,128)(2,1)S(1)}, u32[]{:S(2)}, u32[]{:S(2)}) %all-to-all-start.1) | async-done | bytes 524320 | tf_op jit(solution)/shard_map/all_to_all | solution.py:160
  70.2 5.5 all-to-all-start.4
  78.3 20.8 %all-to-all-done.4 = bf16[128,16,128]{0,2,1:T(8,128)(2,1)S(1)} async-done(((bf16[128,16,128]{0,2,1:T(8,128)(2,1)}), bf16[128,16,128]{0,2,1:T(8,128)(2,1)S(1)}, u32[]{:S(2)}, u32[]{:S(2)}) %all-to-all-start.4) | async-done | bytes 524320 | tf_op jit(solution)/shard_map/all_to_all | solution.py:161
  99.1 4.2 all-to-all-start.2
  103.4 2.5 scatter_custom_fusion.1
  106.7 6.0 all-to-all-done.2
  112.8 4.1 all-to-all-start.3
  117.7 13.1 %while.25 = (s32[]{:T(128)}, bf16[4,512,1,128]{3,1,2,0:T(8,128)(2,1)}, bf16[4,512,1,128]{3,1,2,0:T(8,128)(2,1)S(1)}, bf16[2048,1,128]{2,0,1:T(8,128)(2,1)S(1)}, bf16[2048,1,128]{2,0,1:T(8,128)(2,1)S(1)}, /*index=5*/s32[]{:T(128)}) while((s32[]{:T(128)}, bf16[4,512,1,128]{3,1,2,0:T(8,128)(2,1)}, bf16[4,512,1,128]{3,1,2,0:T(8,128)(2,1)S(1)}, ...), condition=%wide.region_10.11_spmd, body=%wide.region_7.10_spmd.sunk | while | flops 546372608 | bytes 13904457 | solution.py:67
  130.8 11.7 %all-to-all-done.3 = bf16[16,16,1536]{2,1,0:T(8,128)(2,1)S(1)} async-done(((bf16[16,16,1536]{2,1,0:T(8,128)(2,1)}), bf16[16,16,1536]{2,1,0:T(8,128)(2,1)S(1)}, u32[]{:S(2)}, u32[]{:S(2)}) %all-to-all-start.3) | async-done | bytes 786464 | tf_op jit(solution)/shard_map/all_to_all | solution.py:137
  142.5 4.9 all-to-all-start.5
  149.5 2.5 scatter_custom_fusion.2
  152.0 15.6 %all-to-all-done.5 = bf16[16,128,128]{2,1,0:T(8,128)(2,1)} async-done(((bf16[16,128,128]{2,1,0:T(8,128)(2,1)}), bf16[16,128,128]{2,1,0:T(8,128)(2,1)}, u32[]{:S(2)}, u32[]{:S(2)}) %all-to-all-start.5) | async-done | bytes 524320 | tf_op jit(solution)/shard_map/all_to_all | solution.py:171
  170.5 2.4 reshape.419
  172.9 7.7 %reshape.446 = bf16[16,262144]{1,0:T(8,128)(2,1)} reshape(bf16[4194304]{0:T(1024)(128)(2,1)} %all-gather.3.cloned.1.call-done) | data formatting | bytes 16777216 | tf_op jit(solution)/shard_map/all_gather | solution.py:21
  180.5 4.7 slice.18
  186.7 1.9 slice.19
  189.9 4.8 reshape_reshape.18
  194.7 4.1 reshape_reshape.19
  200.4 3.2 fusion.58
  209.7 4.2 convolution_convert_fusion.1
  214.9 4.8 all-to-all-start.6
  219.9 4.3 convolution_convert_fusion.2
  224.2 9.3 %all-to-all-done.6 = bf16[128,16,128]{2,0,1:T(8,128)(2,1)} async-done(((bf16[128,16,128]{2,0,1:T(8,128)(2,1)}), bf16[128,16,128]{2,0,1:T(8,128)(2,1)}, u32[]{:S(2)}, u32[]{:S(2)}) %all-to-all-start.6) | async-done | bytes 524320 | tf_op jit(solution)/shard_map/all_to_all | solution.py:201
  234.4 51.8 %while.26 = (s32[]{:T(128)}, f32[2048,1,128]{0,2,1:T(8,128)S(1)}, f32[2048,1,128]{0,2,1:T(8,128)S(1)}, bf16[4,512,1,128]{3,1,2,0:T(8,128)(2,1)}, bf16[4,512,1,12...) while((s32[]{:T(128)}, f32[2048,1,128]{0,2,1:T(8,128)S(1)}, ...), condition=%wide.region_18.19_spmd.clone, body=%wide.region_14.18_spmd.clone.sunk | while | flops 1365309952 | bytes 77749960 | solution.py:97
  235.2 2.0 copy-done
  238.0 3.6 fusion.117
  241.7 2.2 multiply_reduce_fusion.9
  248.1 2.0 copy-done
  250.9 3.7 fusion.117
  254.6 2.2 multiply_reduce_fusion.9
  261.1 2.0 copy-done
  263.9 3.7 fusion.117
  267.6 2.2 multiply_reduce_fusion.9
  274.0 2.0 copy-done
  276.8 3.7 fusion.117
  280.5 2.2 multiply_reduce_fusion.9
  287.3 4.5 all-to-all-start.8
  292.1 14.2 %all-to-all-done.8 = bf16[16,128,128]{2,1,0:T(8,128)(2,1)S(1)} async-done(((bf16[16,128,128]{2,1,0:T(8,128)(2,1)}), bf16[16,128,128]{2,1,0:T(8,128)(2,1)S(1)}, u32[]{:S(2)}, u32[]{:S(2)}) %all-to-all-start.8) | async-done | bytes 524320 | tf_op jit(solution)/shard_map/all_to_all | solution.py:207
  306.3 17.9 %all_to_all.133 = bf16[16,128,128]{2,1,0:T(8,128)(2,1)S(1)} all-to-all(bf16[16,128,128]{2,1,0:T(8,128)(2,1)S(1)} %bitcast.232), channel_id=1, replica_groups=mesh['dp'=16,'seq'=16] {'seq'}, dimensions={0} | all-to-all | bytes 1048576 | tf_op jit(solution)/shard_map/all_to_all | solution.py:208
  324.2 4.5 all-to-all-start.7
  328.8 82.0 %reduce-scatter.8.cloned.1.call-done = bf16[64,1536]{1,0:T(8,128)(2,1)} async-done(((bf16[1024,1536]{1,0:T(8,128)(2,1)}), bf16[64,1536]{1,0:T(8,128)(2,1)}) %reduce-scatter.8.cloned.1.call-update) | async-done | bytes 196624 | tf_op jit(solution)/shard_map/reduce_scatter | solution.py:217
  410.8 92.8 %reduce-scatter.6.cloned.1.call-done = bf16[128,1024]{1,0:T(8,128)(2,1)} async-done(((bf16[2048,1024]{1,0:T(8,128)(2,1)}), bf16[128,1024]{1,0:T(8,128)(2,1)}) %reduce-scatter.6.cloned.1.call-update) | async-done | bytes 262160 | tf_op jit(solution)/shard_map/reduce_scatter | solution.py:214
  507.6 183.5 %all-reduce.3.cloned.1.call-done = (bf16[16,2048]{1,0:T(8,128)(2,1)}, bf16[128,1024]{1,0:T(8,128)(2,1)}, bf16[64,1536]{1,0:T(8,128)(2,1)}) async-done(((bf16[16,2048]{1,0:T(8,128)(2,1)}, bf16[128,1024]{1,0:T(8,128)(2,1)}, bf16[64,1536]{1,0:T(8,128)(2,1)}), (bf16[16,2048]{1,0:T(8,128)(2,1)}, bf16[128,1024]{1,0:T(8,128)(2,1)}, bf16[64,1536]{1,0:T(8,128)(2,1)})) %all-reduce.3.cloned.1.call-update) | async-done | bytes 524304 | tf_op jit(solution)/shard_map/psum | solution.py:222
  691.0 1.8 convert_element_type.186
  (148 shorter events, 68.9 us)
Async XLA Ops:
  7.2 18.8 %copy-start.8 = (bf16[1,128,2048]{2,1,0:T(8,128)(2,1)S(1)}, bf16[1,128,2048]{2,1,0:T(8,128)(2,1)}, u32[]{:S(2)}) copy-start(bf16[1,128,2048]{2,1,0:T(8,128)(2,1)} %param.17) | copy-start | bytes 1572868
  7.2 44.9 %copy-start.9 = (bf16[1,128,2048]{2,1,0:T(8,128)(2,1)S(1)}, bf16[1,128,2048]{2,1,0:T(8,128)(2,1)}, u32[]{:S(2)}) copy-start(bf16[1,128,2048]{2,1,0:T(8,128)(2,1)} %param.18) | copy-start | bytes 1572868
  7.2 45.9 %copy-start.15 = (s32[1,128]{1,0:T(1,128)S(1)}, s32[1,128]{1,0:T(1,128)}, u32[]{:S(2)}) copy-start(s32[1,128]{1,0:T(1,128)} %param.23) | copy-start | bytes 1540
  7.2 165.7 %all-gather.3.cloned.1.call-start = ((), (), s32[]{:S(2)}) async-start(), calls=%async_computation.16 | async-start | bytes 8912896 | tf_op jit(solution)/shard_map/all_gather | solution.py:21
  9.5 68.4 %copy-start.5 = (bf16[1,128,1536]{2,1,0:T(8,128)(2,1)S(1)}, bf16[1,128,1536]{2,1,0:T(8,128)(2,1)}, u32[]{:S(2)}) copy-start(bf16[1,128,1536]{2,1,0:T(8,128)(2,1)} %param.20) | copy-start | bytes 1179652
  11.2 92.2 %copy-start.13 = (f32[1536]{0:T(1024)S(1)}, f32[1536]{0:T(1024)}, u32[]{:S(2)}) copy-start(f32[1536]{0:T(1024)} %param.22) | copy-start | bytes 18436
  11.2 92.2 %copy-start.14 = (f32[1536]{0:T(1024)S(1)}, f32[1536]{0:T(1024)}, u32[]{:S(2)}) copy-start(f32[1536]{0:T(1024)} %param.21) | copy-start | bytes 18436
  13.3 34.3 %all-to-all-start = ((bf16[128,16,128]{0,2,1:T(8,128)(2,1)}), bf16[128,16,128]{0,2,1:T(8,128)(2,1)S(1)}, u32[]{:S(2)}, u32[]{:S(2)}) async-start(bf16[128,16,128]{0,2,1:T(8,128)(2,1)} %bitcast.7), calls=%async_computation | async-start | bytes 1048576 | tf_op jit(solution)/shard_map/all_to_all | solution.py:159
  47.6 22.6 %all-to-all-start.1 = ((bf16[128,16,128]{0,2,1:T(8,128)(2,1)}), bf16[128,16,128]{0,2,1:T(8,128)(2,1)S(1)}, u32[]{:S(2)}, u32[]{:S(2)}) async-start(bf16[128,16,128]{0,2,1:T(8,128)(2,1)} %bitcast.11), calls=%async_computation.1 | async-start | bytes 1048576 | tf_op jit(solution)/shard_map/all_to_all | solution.py:160
  70.2 28.9 %all-to-all-start.4 = ((bf16[128,16,128]{0,2,1:T(8,128)(2,1)}), bf16[128,16,128]{0,2,1:T(8,128)(2,1)S(1)}, u32[]{:S(2)}, u32[]{:S(2)}) async-start(bf16[128,16,128]{0,2,1:T(8,128)(2,1)} %bitcast.25), calls=%async_computation.4 | async-start | bytes 1048576 | tf_op jit(solution)/shard_map/all_to_all | solution.py:161
  99.1 13.6 %all-to-all-start.2 = ((s32[16,1,16]{2,1,0:T(1,128)}), s32[16,1,16]{2,1,0:T(1,128)S(1)}, u32[]{:S(2)}, u32[]{:S(2)}) async-start(s32[16,1,16]{2,1,0:T(1,128)} %all_to_all.105), calls=%async_computation.2 | async-start | bytes 16384 | tf_op jit(solution)/shard_map/all_to_all | solution.py:144
  112.8 29.7 %all-to-all-start.3 = ((bf16[16,16,1536]{2,1,0:T(8,128)(2,1)}), bf16[16,16,1536]{2,1,0:T(8,128)(2,1)S(1)}, u32[]{:S(2)}, u32[]{:S(2)}) async-start(bf16[16,16,1536]{2,1,0:T(8,128)(2,1)} %bitcast.22), calls=%async_computation.3 | async-start | bytes 1572864 | tf_op jit(solution)/shard_map/all_to_all | solution.py:137
  130.8 21.2 %copy-start.10 = (bf16[2048,1,128]{2,0,1:T(8,128)(2,1)}, bf16[2048,1,128]{2,0,1:T(8,128)(2,1)S(1)}, u32[]{:S(2)}) copy-start(bf16[2048,1,128]{2,0,1:T(8,128)(2,1)S(1)} %get-tuple-element.385) | copy-start | bytes 1572868
  142.5 25.0 %all-to-all-start.5 = ((bf16[16,128,128]{2,1,0:T(8,128)(2,1)}), bf16[16,128,128]{2,1,0:T(8,128)(2,1)}, u32[]{:S(2)}, u32[]{:S(2)}) async-start(bf16[16,128,128]{2,1,0:T(8,128)(2,1)} %bitcast.28), calls=%async_computation.5 | async-start | bytes 1048576 | tf_op jit(solution)/shard_map/all_to_all | solution.py:171
  147.5 181.4 %reduce-scatter.4.cloned.1.call-start = ((), (), s32[]{:S(2)}) async-start(), calls=%async_computation.13 | async-start | bytes 1114112 | tf_op jit(solution)/shard_map/reduce_scatter | solution.py:211
  180.5 6.2 copy-start.3
  186.7 1.9 slice-start
  194.7 5.7 copy-start.4
  198.8 4.9 copy-start.6
  198.8 4.9 copy-start.12
  204.4 1.3 copy-start.16
  204.4 2.5 copy-start.2
  209.7 201.1 %reduce-scatter.8.cloned.1.call-start = ((), (), s32[]{:S(2)}) async-start(), calls=%async_computation.15 | async-start | bytes 3342336 | tf_op jit(solution)/shard_map/reduce_scatter | solution.py:217
  214.9 18.6 %all-to-all-start.6 = ((bf16[128,16,128]{2,0,1:T(8,128)(2,1)}), bf16[128,16,128]{2,0,1:T(8,128)(2,1)}, u32[]{:S(2)}, u32[]{:S(2)}) async-start(bf16[128,16,128]{2,0,1:T(8,128)(2,1)} %bitcast.194), calls=%async_computation.6 | async-start | bytes 1048576 | tf_op jit(solution)/shard_map/all_to_all | solution.py:201
  219.6 284.0 %reduce-scatter.6.cloned.1.call-start = ((), (), s32[]{:S(2)}) async-start(), calls=%async_computation.14 | async-start | bytes 4456448 | tf_op jit(solution)/shard_map/reduce_scatter | solution.py:214
  224.2 10.2 %copy-start.7 = (f32[2048,1,128]{0,2,1:T(8,128)S(1)}, f32[2048,1,128]{0,2,1:T(8,128)}, u32[]{:S(2)}) copy-start(f32[2048,1,128]{0,2,1:T(8,128)} %custom-call.1) | copy-start | bytes 3145732
  235.2 2.0 copy-start
  238.0 3.7 copy-start.1
  238.0 3.7 copy-start.11
  248.1 2.0 copy-start
  250.9 3.7 copy-start.1
  250.9 3.7 copy-start.11
  261.1 2.0 copy-start
  263.9 3.7 copy-start.1
  263.9 3.7 copy-start.11
  274.0 2.0 copy-start
  276.8 3.7 copy-start.1
  276.8 3.7 copy-start.11
  287.3 19.0 %all-to-all-start.8 = ((bf16[16,128,128]{2,1,0:T(8,128)(2,1)}), bf16[16,128,128]{2,1,0:T(8,128)(2,1)S(1)}, u32[]{:S(2)}, u32[]{:S(2)}) async-start(bf16[16,128,128]{2,1,0:T(8,128)(2,1)} %bitcast.37), calls=%async_computation.8 | async-start | bytes 1048576 | tf_op jit(solution)/shard_map/all_to_all | solution.py:207
  324.2 182.0 %all-to-all-start.7 = ((bf16[16,128,128]{2,1,0:T(8,128)(2,1)}), bf16[16,128,128]{2,1,0:T(8,128)(2,1)S(1)}, u32[]{:S(2)}, u32[]{:S(2)}) async-start(bf16[16,128,128]{2,1,0:T(8,128)(2,1)} %bitcast.34), calls=%async_computation.7 | async-start | bytes 1048576 | tf_op jit(solution)/shard_map/all_to_all | solution.py:206
  328.8 362.3 %all-reduce.3.cloned.1.call-start = ((), (), s32[]{:S(2)}) async-start(), calls=%async_computation.17 | async-start | bytes 1048576 | tf_op jit(solution)/shard_map/psum | solution.py:222
Sparse Core Ops, SparseCore 0:
  11.4 155.1 all-gather.2
  209.8 102.7 reduce-scatter.3
  315.3 95.4 reduce-scatter.7
  413.4 90.2 reduce-scatter.5
  506.6 184.4 all-reduce.2
where the time goes:
time: 704 us; the launch traced here: 703 us
  waiting for transfers between devices  474 us (67%)
  matrix products  61 us (9%)
  local copies, waits for them, and re-layouts  59.7 us (8%)
  starting transfers between devices  50.1 us (7%)
  other arithmetic  25 us (4%)
  blocking collectives  17.9 us (3%)
  between operations  14.7 us (2%)
    psum x1, waiting for transfers between devices, shards(): lax.psum(share_gate.astype(jnp.bfloat16), 'seq').astype(jnp.float32)  183 us
    reduce_scatter x1, waiting for transfers between devices, shards(): lax.psum_scatter(part_lift.astype(jnp.bfloat16), 'dp', scatter_dimension=...  92.8 us
    reduce_scatter x1, waiting for transfers between devices, shards(): lax.psum_scatter(part_out.astype(jnp.bfloat16), 'dp', scatter_dimension=0...  82 us
    all_to_all x1, waiting for transfers between devices, shards(): lax.all_to_all(value_states[0], 'seq', split_axis=1, concat_axis=0, tiled...  20.8 us
    all_to_all x1, waiting for transfers between devices, shards(): lax.all_to_all(queries[0], 'seq', split_axis=1, concat_axis=0, tiled=True)  20.7 us
    all_to_all x1, blocking collectives, shards(): lax.all_to_all(grad_value, 'seq', split_axis=0, concat_axis=1, tiled=True)  17.9 us
    all_to_all x1, waiting for transfers between devices, shards(): lax.all_to_all(key_states[0], 'seq', split_axis=1, concat_axis=0, tiled=T...  17.1 us
    all_to_all x1, waiting for transfers between devices, shards(): lax.all_to_all(mixed_heads, 'seq', split_axis=0, concat_axis=1, tiled=True)  15.6 us
  transfers between devices with their start and end apart: 14, of which 11 were waited for; matrix products, arithmetic and copies ran while one was open for 13% of the time, Pallas kernels for 0%

commit v1 on v0

--- a/solution.py
+++ b/solution.py
@@ -219,7 +219,7 @@
         ).astype(jnp.float32),
     )
     grad_gate, grad_lift, grad_out = (
-        lax.psum(share_gate.astype(jnp.bfloat16), "seq").astype(jnp.float32),
+        jnp.sum(lax.all_gather(share_gate.astype(jnp.bfloat16), "seq"), axis=0).astype(jnp.float32),
         lax.psum(share_lift.astype(jnp.bfloat16), "seq").astype(jnp.float32),
         lax.psum(share_out.astype(jnp.bfloat16), "seq").astype(jnp.float32),
     )

time: 704 us -> 755 us (1.072)
  waiting for transfers between devices: 474 us -> 504 us
  blocking collectives: 17.9 us -> 32.1 us
    all_gather x0 -> x1, waiting for transfers between devices: none -> 62.1 us  [shards(): lax.all_gather(share_gate.astype(jnp.bfloat16), 'seq')]
    reduce_scatter x1, waiting for transfers between devices: 82 us -> 58.2 us  [shards(): lax.psum_scatter(part_out.astype(jnp.bfloat16), 'dp', scatter_dimension=0...]
    reduce_scatter x1, waiting for transfers between devices: 0.02 us -> 20.8 us  [shards(): lax.psum_scatter(part_gate.astype(jnp.bfloat16), 'dp', scatter_dimension=...]
    all_to_all x1, waiting for transfers between devices: 14.2 us -> 0.01 us  [shards(): lax.all_to_all(grad_key, 'seq', split_axis=0, concat_axis=1, tiled=True)]
    all_to_all x1, blocking collectives: 17.9 us -> 32.1 us  [shards(): lax.all_to_all(grad_value, 'seq', split_axis=0, concat_axis=1, tiled=True)]
    psum x1, waiting for transfers between devices: 183 us -> 170 us  [shards(): lax.psum(share_lift.astype(jnp.bfloat16), 'seq').astype(jnp.float32)]
  transfers between devices with their start and end apart: 14 -> 15, of which waited for: 11 -> 12; matrix products, arithmetic and copies ran while one was open for 13% -> 12% of each run, Pallas kernels for 0% -> 0%
where the time goes in v1:
time: 755 us; the launch traced here: 752 us
  waiting for transfers between devices  504 us (67%)
  matrix products  61 us (8%)
  local copies, waits for them, and re-layouts  59.7 us (8%)
  starting transfers between devices  55.1 us (7%)
  blocking collectives  32.1 us (4%)
  other arithmetic  25.6 us (3%)
  between operations  15.1 us (2%)
    psum x1, waiting for transfers between devices, shards(): lax.psum(share_lift.astype(jnp.bfloat16), 'seq').astype(jnp.float32)  170 us
    reduce_scatter x1, waiting for transfers between devices, shards(): lax.psum_scatter(part_lift.astype(jnp.bfloat16), 'dp', scatter_dimension=...  91.3 us
    all_gather x1, waiting for transfers between devices, shards(): lax.all_gather(share_gate.astype(jnp.bfloat16), 'seq')  62.1 us
    reduce_scatter x1, waiting for transfers between devices, shards(): lax.psum_scatter(part_out.astype(jnp.bfloat16), 'dp', scatter_dimension=0...  58.2 us
    all_to_all x1, blocking collectives, shards(): lax.all_to_all(grad_value, 'seq', split_axis=0, concat_axis=1, tiled=True)  32.1 us
    all_to_all x1, waiting for transfers between devices, shards(): lax.all_to_all(value_states[0], 'seq', split_axis=1, concat_axis=0, tiled...  20.8 us
    reduce_scatter x1, waiting for transfers between devices, shards(): lax.psum_scatter(part_gate.astype(jnp.bfloat16), 'dp', scatter_dimension=...  20.8 us
    all_to_all x1, waiting for transfers between devices, shards(): lax.all_to_all(queries[0], 'seq', split_axis=1, concat_axis=0, tiled=True)  20.7 us
  transfers between devices with their start and end apart: 15, of which 12 were waited for; matrix products, arithmetic and copies ran while one was open for 12% of the time, Pallas kernels for 0%

profile of v1, /device:TPU:1, one launch (start us, length us, event | category | flops | bytes accessed | tf_op | source)
XLA Modules:
  0.0 752.5 jit_solution(14621622369834452405)
XLA Ops:
  11.3 2.0 copy.82
  13.3 12.6 %all-to-all-start = ((bf16[128,16,128]{0,2,1:T(8,128)(2,1)}), bf16[128,16,128]{0,2,1:T(8,128)(2,1)S(1)}, u32[]{:S(2)}, u32[]{:S(2)}) async-start(bf16[128,16,128]{0,2,1:T(8,128)(2,1)} %bitcast.7), calls=%async_computation | async-start | bytes 1048576 | tf_op jit(solution)/shard_map/all_to_all | solution.py:159
  26.9 20.7 %all-to-all-done = bf16[128,16,128]{0,2,1:T(8,128)(2,1)S(1)} async-done(((bf16[128,16,128]{0,2,1:T(8,128)(2,1)}), bf16[128,16,128]{0,2,1:T(8,128)(2,1)S(1)}, u32[]{:S(2)}, u32[]{:S(2)}) %all-to-all-start) | async-done | bytes 524320 | tf_op jit(solution)/shard_map/all_to_all | solution.py:159
  47.6 4.5 all-to-all-start.1
  53.1 17.1 %all-to-all-done.1 = bf16[128,16,128]{0,2,1:T(8,128)(2,1)S(1)} async-done(((bf16[128,16,128]{0,2,1:T(8,128)(2,1)}), bf16[128,16,128]{0,2,1:T(8,128)(2,1)S(1)}, u32[]{:S(2)}, u32[]{:S(2)}) %all-to-all-start.1) | async-done | bytes 524320 | tf_op jit(solution)/shard_map/all_to_all | solution.py:160
  70.2 5.5 all-to-all-start.4
  78.3 20.8 %all-to-all-done.4 = bf16[128,16,128]{0,2,1:T(8,128)(2,1)S(1)} async-done(((bf16[128,16,128]{0,2,1:T(8,128)(2,1)}), bf16[128,16,128]{0,2,1:T(8,128)(2,1)S(1)}, u32[]{:S(2)}, u32[]{:S(2)}) %all-to-all-start.4) | async-done | bytes 524320 | tf_op jit(solution)/shard_map/all_to_all | solution.py:161
  99.1 4.2 all-to-all-start.2
  103.4 2.5 scatter_custom_fusion.1
  106.7 6.0 all-to-all-done.2
  112.8 4.1 all-to-all-start.3
  117.7 13.1 %while.25 = (s32[]{:T(128)}, bf16[4,512,1,128]{3,1,2,0:T(8,128)(2,1)}, bf16[4,512,1,128]{3,1,2,0:T(8,128)(2,1)S(1)}, bf16[2048,1,128]{2,0,1:T(8,128)(2,1)S(1)}, bf16[2048,1,128]{2,0,1:T(8,128)(2,1)S(1)}, /*index=5*/s32[]{:T(128)}) while((s32[]{:T(128)}, bf16[4,512,1,128]{3,1,2,0:T(8,128)(2,1)}, bf16[4,512,1,128]{3,1,2,0:T(8,128)(2,1)S(1)}, ...), condition=%wide.region_10.11_spmd, body=%wide.region_7.10_spmd.sunk | while | flops 546372608 | bytes 13904457 | solution.py:67
  130.8 11.7 %all-to-all-done.3 = bf16[16,16,1536]{2,1,0:T(8,128)(2,1)S(1)} async-done(((bf16[16,16,1536]{2,1,0:T(8,128)(2,1)}), bf16[16,16,1536]{2,1,0:T(8,128)(2,1)S(1)}, u32[]{:S(2)}, u32[]{:S(2)}) %all-to-all-start.3) | async-done | bytes 786464 | tf_op jit(solution)/shard_map/all_to_all | solution.py:137
  142.5 4.9 all-to-all-start.5
  149.5 2.5 scatter_custom_fusion.2
  152.0 15.6 %all-to-all-done.5 = bf16[16,128,128]{2,1,0:T(8,128)(2,1)} async-done(((bf16[16,128,128]{2,1,0:T(8,128)(2,1)}), bf16[16,128,128]{2,1,0:T(8,128)(2,1)}, u32[]{:S(2)}, u32[]{:S(2)}) %all-to-all-start.5) | async-done | bytes 524320 | tf_op jit(solution)/shard_map/all_to_all | solution.py:171
  170.5 2.4 reshape.419
  172.9 7.7 %reshape.446 = bf16[16,262144]{1,0:T(8,128)(2,1)} reshape(bf16[4194304]{0:T(1024)(128)(2,1)} %all-gather.5.cloned.1.call-done) | data formatting | bytes 16777216 | tf_op jit(solution)/shard_map/all_gather | solution.py:21
  180.5 4.7 slice.18
  186.7 1.9 slice.19
  189.9 4.8 reshape_reshape.18
  194.7 4.1 reshape_reshape.19
  200.4 3.2 fusion.58
  209.7 4.2 convolution_convert_fusion.1
  214.9 4.8 all-to-all-start.6
  219.9 4.3 convolution_convert_fusion.2
  224.2 9.3 %all-to-all-done.6 = bf16[128,16,128]{2,0,1:T(8,128)(2,1)} async-done(((bf16[128,16,128]{2,0,1:T(8,128)(2,1)}), bf16[128,16,128]{2,0,1:T(8,128)(2,1)}, u32[]{:S(2)}, u32[]{:S(2)}) %all-to-all-start.6) | async-done | bytes 524320 | tf_op jit(solution)/shard_map/all_to_all | solution.py:201
  234.4 51.8 %while.26 = (s32[]{:T(128)}, f32[2048,1,128]{0,2,1:T(8,128)S(1)}, f32[2048,1,128]{0,2,1:T(8,128)S(1)}, bf16[4,512,1,128]{3,1,2,0:T(8,128)(2,1)}, bf16[4,512,1,12...) while((s32[]{:T(128)}, f32[2048,1,128]{0,2,1:T(8,128)S(1)}, ...), condition=%wide.region_18.19_spmd.clone, body=%wide.region_14.18_spmd.clone.sunk | while | flops 1365309952 | bytes 77749960 | solution.py:97
  235.2 2.0 copy-done
  238.0 3.6 fusion.117
  241.7 2.2 multiply_reduce_fusion.9
  248.1 2.0 copy-done
  250.9 3.7 fusion.117
  254.6 2.2 multiply_reduce_fusion.9
  261.1 2.0 copy-done
  263.9 3.7 fusion.117
  267.6 2.2 multiply_reduce_fusion.9
  274.0 2.0 copy-done
  276.8 3.7 fusion.117
  280.5 2.2 multiply_reduce_fusion.9
  287.3 4.5 all-to-all-start.8
  291.8 20.8 %reduce-scatter.4.cloned.1.call-done = bf16[16,2048]{1,0:T(8,128)(2,1)} async-done(((bf16[256,2048]{1,0:T(8,128)(2,1)}), bf16[16,2048]{1,0:T(8,128)(2,1)}) %reduce-scatter.4.cloned.1.call-update) | async-done | bytes 65552 | tf_op jit(solution)/shard_map/reduce_scatter | solution.py:211
  313.0 32.1 %all_to_all.133 = bf16[16,128,128]{2,1,0:T(8,128)(2,1)S(1)} all-to-all(bf16[16,128,128]{2,1,0:T(8,128)(2,1)S(1)} %bitcast.233), channel_id=1, replica_groups=mesh['dp'=16,'seq'=16] {'seq'}, dimensions={0} | all-to-all | bytes 1048576 | tf_op jit(solution)/shard_map/all_to_all | solution.py:208
  345.0 9.5 %all-to-all-start.7 = ((bf16[16,128,128]{2,1,0:T(8,128)(2,1)}), bf16[16,128,128]{2,1,0:T(8,128)(2,1)S(1)}, u32[]{:S(2)}, u32[]{:S(2)}) async-start(bf16[16,128,128]{2,1,0:T(8,128)(2,1)} %bitcast.34), calls=%async_computation.7 | async-start | bytes 1048576 | tf_op jit(solution)/shard_map/all_to_all | solution.py:206
  354.6 58.2 %reduce-scatter.8.cloned.1.call-done = bf16[64,1536]{1,0:T(8,128)(2,1)} async-done(((bf16[1024,1536]{1,0:T(8,128)(2,1)}), bf16[64,1536]{1,0:T(8,128)(2,1)}) %reduce-scatter.8.cloned.1.call-update) | async-done | bytes 196624 | tf_op jit(solution)/shard_map/reduce_scatter | solution.py:217
  412.8 91.3 %reduce-scatter.6.cloned.1.call-done = bf16[128,1024]{1,0:T(8,128)(2,1)} async-done(((bf16[2048,1024]{1,0:T(8,128)(2,1)}), bf16[128,1024]{1,0:T(8,128)(2,1)}) %reduce-scatter.6.cloned.1.call-update) | async-done | bytes 262160 | tf_op jit(solution)/shard_map/reduce_scatter | solution.py:214
  508.0 62.1 %all-gather.7.cloned.1.call-done = bf16[256,2048]{1,0:T(8,128)(2,1)} async-done(((bf16[16,2048]{1,0:T(8,128)(2,1)}), bf16[256,2048]{1,0:T(8,128)(2,1)}) %all-gather.7.cloned.1.call-update) | async-done | bytes 1048592 | tf_op jit(solution)/shard_map/all_gather | solution.py:222
  572.2 169.9 %all-reduce.3.cloned.1.call-done = (bf16[128,1024]{1,0:T(8,128)(2,1)}, bf16[64,1536]{1,0:T(8,128)(2,1)}) async-done(((bf16[128,1024]{1,0:T(8,128)(2,1)}, bf16[64,1536]{1,0:T(8,128)(2,1)}), (bf16[128,1024]{1,0:T(8,128)(2,1)}, bf16[64,1536]{1,0:T(8,128)(2,1)})) %all-reduce.3.cloned.1.call-update) | async-done | bytes 458768 | tf_op jit(solution)/shard_map/psum | solution.py:223
  (152 shorter events, 71.3 us)
Async XLA Ops:
  7.2 18.8 %copy-start.8 = (bf16[1,128,2048]{2,1,0:T(8,128)(2,1)S(1)}, bf16[1,128,2048]{2,1,0:T(8,128)(2,1)}, u32[]{:S(2)}) copy-start(bf16[1,128,2048]{2,1,0:T(8,128)(2,1)} %param.17) | copy-start | bytes 1572868
  7.2 44.9 %copy-start.9 = (bf16[1,128,2048]{2,1,0:T(8,128)(2,1)S(1)}, bf16[1,128,2048]{2,1,0:T(8,128)(2,1)}, u32[]{:S(2)}) copy-start(bf16[1,128,2048]{2,1,0:T(8,128)(2,1)} %param.18) | copy-start | bytes 1572868
  7.2 45.9 %copy-start.15 = (s32[1,128]{1,0:T(1,128)S(1)}, s32[1,128]{1,0:T(1,128)}, u32[]{:S(2)}) copy-start(s32[1,128]{1,0:T(1,128)} %param.23) | copy-start | bytes 1540
  7.2 165.7 %all-gather.5.cloned.1.call-start = ((), (), s32[]{:S(2)}) async-start(), calls=%async_computation.16 | async-start | bytes 8912896 | tf_op jit(solution)/shard_map/all_gather | solution.py:21
  9.5 68.4 %copy-start.5 = (bf16[1,128,1536]{2,1,0:T(8,128)(2,1)S(1)}, bf16[1,128,1536]{2,1,0:T(8,128)(2,1)}, u32[]{:S(2)}) copy-start(bf16[1,128,1536]{2,1,0:T(8,128)(2,1)} %param.20) | copy-start | bytes 1179652
  11.2 92.2 %copy-start.13 = (f32[1536]{0:T(1024)S(1)}, f32[1536]{0:T(1024)}, u32[]{:S(2)}) copy-start(f32[1536]{0:T(1024)} %param.22) | copy-start | bytes 18436
  11.2 92.2 %copy-start.14 = (f32[1536]{0:T(1024)S(1)}, f32[1536]{0:T(1024)}, u32[]{:S(2)}) copy-start(f32[1536]{0:T(1024)} %param.21) | copy-start | bytes 18436
  13.3 34.3 %all-to-all-start = ((bf16[128,16,128]{0,2,1:T(8,128)(2,1)}), bf16[128,16,128]{0,2,1:T(8,128)(2,1)S(1)}, u32[]{:S(2)}, u32[]{:S(2)}) async-start(bf16[128,16,128]{0,2,1:T(8,128)(2,1)} %bitcast.7), calls=%async_computation | async-start | bytes 1048576 | tf_op jit(solution)/shard_map/all_to_all | solution.py:159
  47.6 22.6 %all-to-all-start.1 = ((bf16[128,16,128]{0,2,1:T(8,128)(2,1)}), bf16[128,16,128]{0,2,1:T(8,128)(2,1)S(1)}, u32[]{:S(2)}, u32[]{:S(2)}) async-start(bf16[128,16,128]{0,2,1:T(8,128)(2,1)} %bitcast.11), calls=%async_computation.1 | async-start | bytes 1048576 | tf_op jit(solution)/shard_map/all_to_all | solution.py:160
  70.2 28.9 %all-to-all-start.4 = ((bf16[128,16,128]{0,2,1:T(8,128)(2,1)}), bf16[128,16,128]{0,2,1:T(8,128)(2,1)S(1)}, u32[]{:S(2)}, u32[]{:S(2)}) async-start(bf16[128,16,128]{0,2,1:T(8,128)(2,1)} %bitcast.25), calls=%async_computation.4 | async-start | bytes 1048576 | tf_op jit(solution)/shard_map/all_to_all | solution.py:161
  99.1 13.6 %all-to-all-start.2 = ((s32[16,1,16]{2,1,0:T(1,128)}), s32[16,1,16]{2,1,0:T(1,128)S(1)}, u32[]{:S(2)}, u32[]{:S(2)}) async-start(s32[16,1,16]{2,1,0:T(1,128)} %all_to_all.105), calls=%async_computation.2 | async-start | bytes 16384 | tf_op jit(solution)/shard_map/all_to_all | solution.py:144
  112.8 29.7 %all-to-all-start.3 = ((bf16[16,16,1536]{2,1,0:T(8,128)(2,1)}), bf16[16,16,1536]{2,1,0:T(8,128)(2,1)S(1)}, u32[]{:S(2)}, u32[]{:S(2)}) async-start(bf16[16,16,1536]{2,1,0:T(8,128)(2,1)} %bitcast.22), calls=%async_computation.3 | async-start | bytes 1572864 | tf_op jit(solution)/shard_map/all_to_all | solution.py:137
  130.8 21.2 %copy-start.10 = (bf16[2048,1,128]{2,0,1:T(8,128)(2,1)}, bf16[2048,1,128]{2,0,1:T(8,128)(2,1)S(1)}, u32[]{:S(2)}) copy-start(bf16[2048,1,128]{2,0,1:T(8,128)(2,1)S(1)} %get-tuple-element.403) | copy-start | bytes 1572868
  142.5 25.0 %all-to-all-start.5 = ((bf16[16,128,128]{2,1,0:T(8,128)(2,1)}), bf16[16,128,128]{2,1,0:T(8,128)(2,1)}, u32[]{:S(2)}, u32[]{:S(2)}) async-start(bf16[16,128,128]{2,1,0:T(8,128)(2,1)} %bitcast.28), calls=%async_computation.5 | async-start | bytes 1048576 | tf_op jit(solution)/shard_map/all_to_all | solution.py:171
  147.5 165.1 %reduce-scatter.4.cloned.1.call-start = ((), (), s32[]{:S(2)}) async-start(), calls=%async_computation.13 | async-start | bytes 1114112 | tf_op jit(solution)/shard_map/reduce_scatter | solution.py:211
  180.5 6.2 copy-start.3
  186.7 1.9 slice-start
  194.7 5.7 copy-start.4
  198.8 4.9 copy-start.6
  198.8 4.9 copy-start.12
  204.4 1.3 copy-start.16
  204.4 2.5 copy-start.2
  209.7 203.1 %reduce-scatter.8.cloned.1.call-start = ((), (), s32[]{:S(2)}) async-start(), calls=%async_computation.15 | async-start | bytes 3342336 | tf_op jit(solution)/shard_map/reduce_scatter | solution.py:217
  214.9 18.6 %all-to-all-start.6 = ((bf16[128,16,128]{2,0,1:T(8,128)(2,1)}), bf16[128,16,128]{2,0,1:T(8,128)(2,1)}, u32[]{:S(2)}, u32[]{:S(2)}) async-start(bf16[128,16,128]{2,0,1:T(8,128)(2,1)} %bitcast.195), calls=%async_computation.6 | async-start | bytes 1048576 | tf_op jit(solution)/shard_map/all_to_all | solution.py:201
  219.6 284.5 %reduce-scatter.6.cloned.1.call-start = ((), (), s32[]{:S(2)}) async-start(), calls=%async_computation.14 | async-start | bytes 4456448 | tf_op jit(solution)/shard_map/reduce_scatter | solution.py:214
  224.2 10.2 %copy-start.7 = (f32[2048,1,128]{0,2,1:T(8,128)S(1)}, f32[2048,1,128]{0,2,1:T(8,128)}, u32[]{:S(2)}) copy-start(f32[2048,1,128]{0,2,1:T(8,128)} %custom-call.1) | copy-start | bytes 3145732
  235.2 2.0 copy-start
  238.0 3.7 copy-start.1
  238.0 3.7 copy-start.11
  248.1 2.0 copy-start
  250.9 3.7 copy-start.1
  250.9 3.7 copy-start.11
  261.1 2.0 copy-start
  263.9 3.7 copy-start.1
  263.9 3.7 copy-start.11
  274.0 2.0 copy-start
  276.8 3.7 copy-start.1
  276.8 3.7 copy-start.11
  287.3 25.7 %all-to-all-start.8 = ((bf16[16,128,128]{2,1,0:T(8,128)(2,1)}), bf16[16,128,128]{2,1,0:T(8,128)(2,1)S(1)}, u32[]{:S(2)}, u32[]{:S(2)}) async-start(bf16[16,128,128]{2,1,0:T(8,128)(2,1)} %bitcast.37), calls=%async_computation.8 | async-start | bytes 1048576 | tf_op jit(solution)/shard_map/all_to_all | solution.py:207
  291.8 278.4 %all-gather.7.cloned.1.call-start = ((), (), s32[]{:S(2)}) async-start(), calls=%async_computation.17 | async-start | bytes 1114112 | tf_op jit(solution)/shard_map/all_gather | solution.py:222
  345.0 161.7 %all-to-all-start.7 = ((bf16[16,128,128]{2,1,0:T(8,128)(2,1)}), bf16[16,128,128]{2,1,0:T(8,128)(2,1)S(1)}, u32[]{:S(2)}, u32[]{:S(2)}) async-start(bf16[16,128,128]{2,1,0:T(8,128)(2,1)} %bitcast.34), calls=%async_computation.7 | async-start | bytes 1048576 | tf_op jit(solution)/shard_map/all_to_all | solution.py:206
  354.6 387.6 %all-reduce.3.cloned.1.call-start = ((), (), s32[]{:S(2)}) async-start(), calls=%async_computation.18 | async-start | bytes 917504 | tf_op jit(solution)/shard_map/psum | solution.py:223
Sparse Core Ops, SparseCore 0:
  11.4 155.1 all-gather.4
  209.8 102.7 reduce-scatter.3
  315.3 97.4 reduce-scatter.7
  415.4 88.7 reduce-scatter.5
  507.1 63.0 all-gather.6
  572.9 169.1 all-reduce.2
